TPU v7x, 32 devices: a whole 2x2x4 slice. The times are simulated.
32 devices in a mesh: groups: 2 (over y), row: 16 (over z, x, core).
Axes of the slice: x: 2, y: 2, z: 4, core: 2. Of those that a mesh axis runs over, the one named last changes fastest.
Arguments:
- homolog_activation: float32 [32, 512, 256], P('groups', 'row'), parts along dimension 0, may hold values from -6 to 6
- homolog_entry_valid: int32 [32, 512], P('groups', 'row'), parts along dimension 0, may hold values 0 or 1
- amino_valid_flags: int32 [1024], P(('groups', 'row')), parts along dimension 0, may hold values 0 or 1
- first_factor_weights: float32 [256, 32], replicated, may hold values from -0.375 to 0.375
- second_factor_weights: float32 [256, 32], replicated, may hold values from -0.375 to 0.375
- final_linear_weights: float32 [1024, 128], replicated, may hold values from -0.1875 to 0.1875
- couple_delta_deriv: float32 [1024, 512, 128], P(('groups', 'row')), parts along dimension 0, may hold values from -6 to 6
Outputs:
- alignment_grad: float32 [32, 512, 256], P('groups', 'row'), parts along dimension 0
- left_weight_grad: float32 [512, 32], P('groups'), parts along dimension 0
- right_weight_grad: float32 [512, 32], P('groups'), parts along dimension 0
- out_weight_grad: float32 [2048, 128], P('groups'), parts along dimension 0
There are 2 independent parts, one for each index of `groups`. A program takes and returns all parts, laid end to end along the dimension named above; an argument that names none is the same for every part. Nothing has to cross between parts.
All inputs are finite; a program needn't handle non-finite values. No bound on the sum of `homolog_entry_valid` or of `amino_valid_flags` on one device may be relied on, other than what follows from the above.
Results may differ from a plain program's by a relative error of at most 0.0003.
Values sent between devices are 32-bit elements; how exact they have to be, the bound alone decides.
A program may use at most 128 MiB of HBM per device.

v0:
```python
import jax
import jax.numpy as jnp
from jax import lax
from jax.sharding import PartitionSpec as P

SPLIT_PIECES = lax.Precision.HIGHEST


def local(
    homolog_activation,
    homolog_entry_valid,
    amino_valid_flags,
    first_factor_weights,
    second_factor_weights,
    final_linear_weights,
    couple_delta_deriv,
):
    rows = couple_delta_deriv.shape[0]
    total = couple_delta_deriv.shape[1]
    homolog_number_here = homolog_activation.shape[0]
    width = first_factor_weights.shape[1]
    pair_width = final_linear_weights.shape[1]
    keep_mask = homolog_entry_valid.astype(jnp.float32).T
    present = amino_valid_flags.astype(jnp.float32)
    homolog_slice_here = jnp.transpose(homolog_activation, (1, 0, 2))
    first_factor_embed = (
        jnp.einsum("plg,gz->plz", homolog_slice_here, first_factor_weights, precision=SPLIT_PIECES)
        * keep_mask[:, :, None]
    )
    second_factor_embed = (
        jnp.einsum("plg,gz->plz", homolog_slice_here, second_factor_weights, precision=SPLIT_PIECES)
        * keep_mask[:, :, None]
    )
    right_flat, keep_all, present_all = (
        lax.all_gather(
            second_factor_embed.reshape(rows, homolog_number_here * width),
            "row",
            axis=0,
            tiled=True,
        ),
        lax.all_gather(keep_mask, "row", axis=0, tiled=True),
        lax.all_gather(present, "row", axis=0, tiled=True),
    )
    right_all = right_flat.reshape(total, homolog_number_here, width)
    count = jnp.dot(
        keep_mask, keep_all.T, precision=SPLIT_PIECES, preferred_element_type=jnp.float32
    )
    factor = present[:, None] * present_all[None, :] / jnp.maximum(count, 1.0)
    scaled = couple_delta_deriv * factor[:, :, None]
    w_three = final_linear_weights.reshape(width, width, pair_width)
    block = min(256, total)
    right_pieces = []
    for begin in range(0, total, block):
        piece = scaled[:, begin : begin + block]
        feats = jnp.einsum("rjk,abk->rjab", piece, w_three, precision=SPLIT_PIECES)
        right_pieces.append(
            jnp.einsum("rjab,rsa->jsb", feats, first_factor_embed, precision=SPLIT_PIECES)
        )
    carried = jnp.einsum("rjk,jsc->rsck", scaled, right_all, precision=SPLIT_PIECES)
    output_grad = jnp.einsum("rsa,rsck->ack", first_factor_embed, carried, precision=SPLIT_PIECES)
    first_factor_embed_deriv = jnp.einsum("rsck,ack->rsa", carried, w_three, precision=SPLIT_PIECES)
    right_terms = jnp.concatenate(right_pieces, axis=0)
    summed = lax.psum(right_terms, "row")
    second_factor_embed_deriv = lax.dynamic_slice_in_dim(
        summed, lax.axis_index("row") * rows, rows, 0
    )
    first_factor_embed_deriv = first_factor_embed_deriv * keep_mask[:, :, None]
    second_factor_embed_deriv = second_factor_embed_deriv * keep_mask[:, :, None]
    alignment_grad = jnp.einsum(
        "gyo,fo->ygf", first_factor_embed_deriv, first_factor_weights, precision=SPLIT_PIECES
    ) + jnp.einsum(
        "gyo,fo->ygf", second_factor_embed_deriv, second_factor_weights, precision=SPLIT_PIECES
    )
    first_operand_array = jnp.einsum(
        "dxb,dxo->bo", homolog_slice_here, first_factor_embed_deriv, precision=SPLIT_PIECES
    )
    second_operand_array = jnp.einsum(
        "dxb,dxo->bo", homolog_slice_here, second_factor_embed_deriv, precision=SPLIT_PIECES
    )
    output_grad_total, left_grad_total, right_grad_total = lax.psum(
        (output_grad.reshape(width * width, pair_width), first_operand_array, second_operand_array),
        "row",
    )
    return (alignment_grad, left_grad_total, right_grad_total, output_grad_total)


def solution(mesh):
    in_specs = (
        P("groups", "row", None),
        P("groups", "row"),
        P(("groups", "row")),
        P(),
        P(),
        P(),
        P(("groups", "row"), None, None),
    )
    out_specs = (P("groups", "row", None), P("groups", None), P("groups", None), P("groups", None))
    return jax.shard_map(local, mesh=mesh, in_specs=in_specs, out_specs=out_specs, check_vma=False)
```

profile of v0, /device:TPU:8, one launch (start us, length us, event | category | flops | bytes accessed | tf_op | source)
XLA Modules:
  0.0 453.5 jit_solution(17768828914577271759)
XLA Ops:
  8.0 1.8 convolution_multiply_fusion.1
  10.7 19.3 %all-gather = f32[16,32,16]{1,2,0:T(8,128)S(1)} all-gather(f32[1,32,16]{1,2,0:T(8,128)S(1)} %get-tuple-element.24), channel_id=1, replica_groups=mesh['groups'=2,'row'=16] {'row'}, dimensions={0}, use_global_device_ids=true | all-gather | bytes 34816 | tf_op jit(solution)/shard_map/all_gather | solution.py:41
  33.4 24.7 %all-reduce = f32[512]{0:T(512)S(1)} all-reduce(f32[512]{0:T(512)S(1)} %convert_dynamic-update-slice_fusion), channel_id=1, replica_groups=mesh['groups'=2,'row'=16] {'row'}, use_global_device_ids=true, to_apply=%add | all-reduce | flops 512 | bytes 4096
  59.0 5.3 %broadcast_multiply_fusion = f32[32,512,128]{2,1,0:T(8,128)S(1)} fusion(f32[32,512,128]{2,1,0:T(8,128)} %param.13, f32[32,512]{1,0:T(8,128)S(1)} %fusion.22), kind=kLoop, calls=%fused_computation.11 | loop fusion | flops 2097152 | bytes 16842752 | tf_op jit(solution)/shard_map/mul | solution.py:49
  64.3 30.6 %fusion.7 = f32[32,256,32,32]{1,2,0,3:T(8,128)} fusion(f32[32,512,128]{2,1,0:T(8,128)S(1)} %broadcast_multiply_fusion, f32[32,32,128,1]{2,1,0,3:T(8,128)S(1)} %bitcast.87), kind=kOutput, calls=%fused_computation.9 | convolution fusion | flops 12884901888 | bytes 38273024 | tf_op jit(solution)/shard_map/rjk,abk->rjab/dot_general | solution.py:55
  95.0 30.8 %fusion.6 = f32[32,256,32,32]{1,2,0,3:T(8,128)} fusion(f32[32,512,128]{2,1,0:T(8,128)S(1)} %broadcast_multiply_fusion, f32[32,32,128,1]{2,1,0,3:T(8,128)S(1)} %bitcast.88), kind=kOutput, calls=%fused_computation.7 | convolution fusion | flops 12884901888 | bytes 38273024 | tf_op jit(solution)/shard_map/rjk,abk->rjab/dot_general | solution.py:55
  126.6 29.3 %convolution_bitcast_fusion.1 = f32[16,256,32]{1,0,2:T(8,128)} fusion(f32[32,16,32,1]{2,1,0,3:T(8,128)S(1)} %fusion.18, f32[32,256,32,32]{1,2,0,3:T(8,128)} %fusion.7), kind=kOutput, calls=%fused_computation.14 | convolution fusion | flops 1610612736 | bytes 34144256 | tf_op jit(solution)/shard_map/rjab,rsa->jsb/dot_general | solution.py:57
  155.9 2.4 copy.68
  158.3 29.5 %convolution_bitcast_fusion = f32[16,256,32]{1,0,2:T(8,128)} fusion(f32[32,16,32,1]{2,1,0,3:T(8,128)S(1)} %fusion.18, f32[32,256,32,32]{1,2,0,3:T(8,128)} %fusion.6), kind=kOutput, calls=%fused_computation.13 | convolution fusion | flops 1610612736 | bytes 34144256 | tf_op jit(solution)/shard_map/rjab,rsa->jsb/dot_general | solution.py:57
  187.9 3.6 copy.70
  191.5 3.8 pad_maximum_fusion
  195.3 1.6 copy.62
  196.9 16.3 %fusion.8 = f32[32,16,32,128]{3,2,0,1:T(8,128)S(1)} fusion(f32[512,16,32,1]{0,2,3,1:T(8,128)S(1)} %bitcast.91, f32[32,512,128]{2,1,0:T(8,128)} %copy-done.2), kind=kOutput, calls=%fused_computation.12 | convolution fusion | flops 12884901888 | bytes 17825792 | tf_op jit(solution)/shard_map/rjk,jsc->rsck/dot_general | solution.py:59
  213.2 3.2 copy-done.1
  216.4 9.4 %fusion.11 = f32[32,32,128]{2,0,1:T(8,128)S(1)} fusion(f32[32,16,32,1]{2,1,0,3:T(8,128)S(1)} %fusion.18, f32[32,16,32,128]{3,2,0,1:T(8,128)S(1)} %fusion.8), kind=kOutput, calls=%fused_computation.15 | convolution fusion | flops 805306368 | bytes 8978432 | tf_op jit(solution)/shard_map/rsa,rsck->ack/dot_general | solution.py:60
  227.0 14.3 %fusion.19 = f32[32,16,32]{2,1,0:T(8,128)S(1)} fusion(f32[32,16,32,128]{3,2,0,1:T(8,128)} %copy-done.1, f32[32,32,128]{2,1,0:T(8,128)S(1)} %bitcast.89, f32[32,16]{1,0:T(8,128)S(1)} %copy.61), kind=kOutput, calls=%fused_computation.22 | convolution fusion | flops 805322752 | bytes 8980480 | tf_op jit(solution)/shard_map/rsck,ack->rsa/dot_general | solution.py:61
  241.3 1.4 convolution_bitcast_fusion.3
  243.3 105.7 %all-reduce.8.cloned.1.call-done = (f32[512,16,32]{2,1,0:T(8,128)}, f32[1024,128]{1,0:T(8,128)}) async-done(((f32[512,16,32]{2,1,0:T(8,128)}, f32[1024,128]{1,0:T(8,128)}), (f32[512,16,32]{2,1,0:T(8,128)}, f32[1024,128]{1,0:T(8,128)})) %all-reduce.8.cloned.1.call-update) | async-done | bytes 1572880 | tf_op jit(solution)/shard_map/psum | solution.py:63
  348.9 2.4 convolution_bitcast_fusion.2
  351.4 1.6 fusion.14
  354.1 88.0 %all-reduce.6.cloned.1.call-done = (f32[256,32]{0,1:T(8,128)}, f32[256,32]{0,1:T(8,128)}) async-done(((f32[256,32]{0,1:T(8,128)}, f32[256,32]{0,1:T(8,128)}), (f32[256,32]{0,1:T(8,128)}, f32[256,32]{0,1:T(8,128)})) %all-reduce.6.cloned.1.call-update) | async-done | bytes 65552 | tf_op jit(solution)/shard_map/psum | solution.py:80
  442.1 1.4 copy.115
  443.5 1.4 copy.116
  444.9 1.9 copy.117
  (32 shorter events, 9.0 us)
Async XLA Ops:
  7.2 118.6 %copy-start = (f32[256,32]{0,1:T(8,128)S(1)}, f32[256,32]{0,1:T(8,128)}, u32[]{:S(2)}) copy-start(f32[256,32]{0,1:T(8,128)} %param.10) | copy-start | bytes 98308
  7.2 188.1 %all-gather.3.cloned.1.call-start = ((), (), s32[]{:S(2)}) async-start(), calls=%async_computation | async-start | bytes 1114112 | tf_op jit(solution)/shard_map/all_gather | solution.py:35
  10.6 338.3 %all-reduce.8.cloned.1.call-start = ((), (), s32[]{:S(2)}) async-start(), calls=%async_computation.2 | async-start | bytes 9437184 | tf_op jit(solution)/shard_map/psum | solution.py:63
  59.0 5.3 %copy-start.4 = (f32[1024,128]{1,0:T(8,128)S(1)}, f32[1024,128]{1,0:T(8,128)}, u32[]{:S(2)}) copy-start(f32[1024,128]{1,0:T(8,128)} %param.12) | copy-start | bytes 1572868
  64.3 30.7 %copy-start.2 = (f32[32,512,128]{2,1,0:T(8,128)}, f32[32,512,128]{2,1,0:T(8,128)S(1)}, u32[]{:S(2)}) copy-start(f32[32,512,128]{2,1,0:T(8,128)S(1)} %broadcast_multiply_fusion) | copy-start | bytes 25165828
  95.0 30.8 %copy-start.3 = (f32[16,32,256]{2,1,0:T(8,128)S(1)}, f32[16,32,256]{2,1,0:T(8,128)}, u32[]{:S(2)}) copy-start(f32[16,32,256]{2,1,0:T(8,128)} %param.7) | copy-start | bytes 1572868
  213.2 3.2 copy-start.1
  227.0 124.4 %copy-start.5 = (f32[256,32]{0,1:T(8,128)S(1)}, f32[256,32]{0,1:T(8,128)}, u32[]{:S(2)}) copy-start(f32[256,32]{0,1:T(8,128)} %param.11) | copy-start | bytes 98308
  227.0 215.1 %all-reduce.6.cloned.1.call-start = ((), (), s32[]{:S(2)}) async-start(), calls=%async_computation.1 | async-start | bytes 131072 | tf_op jit(solution)/shard_map/psum | solution.py:80
Sparse Core Ops, SparseCore 0:
  10.8 38.1 all-gather.2
  227.1 121.7 all-reduce.7
  353.1 89.0 all-reduce.5
where the time goes:
time: 461 us; the launch traced here: 453 us
  waiting for transfers between devices  194 us (42%)
  matrix products  170 us (37%)
  blocking collectives  43.9 us (10%)
  local copies, waits for them, and re-layouts  19.9 us (4%)
  between operations  14.7 us (3%)
  other arithmetic  11.2 us (2%)
    psum x1, waiting for transfers between devices, local(): summed = lax.psum(right_terms, 'row')  106 us
    psum x1, waiting for transfers between devices, local(): lax.psum((output_grad.reshape(width * width, pair_width), first_operand_a...  88 us
    dot_general x2, matrix products, local(): feats = jnp.einsum('rjk,abk->rjab', piece, w_three, precision=SPLIT_PIECES)  61.4 us
    dot_general x2, matrix products, local(): jnp.einsum('rjab,rsa->jsb', feats, first_factor_embed, precision=SPLIT_PI...  58.9 us
    unnamed x1, blocking collectives  24.7 us
    all_gather x1, blocking collectives, local(): lax.all_gather(keep_mask, 'row', axis=0, tiled=True)  19.3 us
    dot_general x1, matrix products, local(): jnp.einsum('rjk,jsc->rsck', scaled, right_all, precision=SPLIT_PIECES)  16.3 us
    dot_general x1, matrix products, local(): jnp.einsum('rsck,ack->rsa', carried, w_three, precision=SPLIT_PIECES)  14.3 us
  transfers between devices with their start and end apart: 3, of which 2 were waited for; matrix products, arithmetic and copies ran while one was open for 35% of the time, Pallas kernels for 0%

commit v1 on v0

--- a/solution.py
+++ b/solution.py
@@ -4,6 +4,18 @@
 from jax.sharding import PartitionSpec as P
 
 SPLIT_PIECES = lax.Precision.HIGHEST
+
+
+def orders_apply(piece_in, mesh_dim):
+    q_n = jax.lax.psum(1, axis_name=mesh_dim)
+    formed, u1 = (piece_in, 0)
+    while 1 << u1 < q_n:
+        carry_in = jax.lax.ppermute(
+            formed, axis_name=mesh_dim, perm=[(h, h ^ 1 << u1) for h in range(q_n)]
+        )
+        formed = formed + carry_in
+        u1 = u1 + 1
+    return formed
 
 
 def local(
@@ -60,7 +72,7 @@
     output_grad = jnp.einsum("rsa,rsck->ack", first_factor_embed, carried, precision=SPLIT_PIECES)
     first_factor_embed_deriv = jnp.einsum("rsck,ack->rsa", carried, w_three, precision=SPLIT_PIECES)
     right_terms = jnp.concatenate(right_pieces, axis=0)
-    summed = lax.psum(right_terms, "row")
+    summed = orders_apply(right_terms, "row")
     second_factor_embed_deriv = lax.dynamic_slice_in_dim(
         summed, lax.axis_index("row") * rows, rows, 0
     )

time: 461 us -> 527 us (1.14)
  waiting for transfers between devices: 194 us -> 229 us
  matrix products: 170 us -> 196 us
  starting transfers between devices: 0.12 us -> 9.6 us
    psum x1 -> x0, waiting for transfers between devices: 106 us -> none  [local(): summed = lax.psum(right_terms, 'row')]
    psum x1 -> x2, waiting for transfers between devices: 88 us -> 179 us  [local(): lax.psum((output_grad.reshape(width * width, pair_width), first_operand_a...]
    ppermute x0 -> x4, waiting for transfers between devices: none -> 38.4 us  [orders_apply(): jax.lax.ppermute(formed, axis_name=mesh_dim, perm=[(h, h ^ 1 << u1) for h...]
    dot_general x2, matrix products: 58.9 us -> 88.7 us  [local(): jnp.einsum('rjab,rsa->jsb', feats, first_factor_embed, precision=SPLIT_PI...]
    all_gather x1, waiting for transfers between devices: 0.01 us -> 11.1 us  [local(): lax.all_gather(second_factor_embed.reshape(rows, homolog_number_here * wi...]
    ppermute x0 -> x4, starting transfers between devices: none -> 9.48 us  [orders_apply(): jax.lax.ppermute(formed, axis_name=mesh_dim, perm=[(h, h ^ 1 << u1) for h...]
    dot_general x2 -> x1, local copies, waits for them, and re-layouts: 6.01 us -> 0.16 us  [local(): jnp.einsum('rsck,ack->rsa', carried, w_three, precision=SPLIT_PIECES)]
  transfers between devices with their start and end apart: 3 -> 7, of which waited for: 2 -> 6; matrix products, arithmetic and copies ran while one was open for 35% -> 10% of each run, Pallas kernels for 0% -> 0%
where the time goes in v1:
time: 527 us; the launch traced here: 521 us
  waiting for transfers between devices  229 us (43%)
  matrix products  196 us (37%)
  blocking collectives  43.7 us (8%)
  local copies, waits for them, and re-layouts  15.8 us (3%)
  between operations  14.8 us (3%)
  other arithmetic  11.8 us (2%)
  starting transfers between devices  9.6 us (2%)
    psum x2, waiting for transfers between devices, local(): lax.psum((output_grad.reshape(width * width, pair_width), first_operand_a...  179 us
    dot_general x2, matrix products, local(): jnp.einsum('rjab,rsa->jsb', feats, first_factor_embed, precision=SPLIT_PI...  88.7 us
    dot_general x2, matrix products, local(): feats = jnp.einsum('rjk,abk->rjab', piece, w_three, precision=SPLIT_PIECES)  60.3 us
    ppermute x4, waiting for transfers between devices, orders_apply(): jax.lax.ppermute(formed, axis_name=mesh_dim, perm=[(h, h ^ 1 << u1) for h...  38.4 us
    unnamed x1, blocking collectives  24.6 us
    all_gather x1, blocking collectives, local(): lax.all_gather(keep_mask, 'row', axis=0, tiled=True)  19.1 us
    dot_general x1, matrix products, local(): jnp.einsum('rjk,jsc->rsck', scaled, right_all, precision=SPLIT_PIECES)  16.6 us
    dot_general x1, matrix products, local(): jnp.einsum('rsa,rsck->ack', first_factor_embed, carried, precision=SPLIT_...  12.7 us
  transfers between devices with their start and end apart: 7, of which 6 were waited for; matrix products, arithmetic and copies ran while one was open for 10% of the time, Pallas kernels for 0%

profile of v1, /device:TPU:8, one launch (start us, length us, event | category | flops | bytes accessed | tf_op | source)
XLA Modules:
  0.0 520.5 jit_solution(4388591096407419124)
XLA Ops:
  8.0 19.1 %all-gather = f32[16,32,16]{1,2,0:T(8,128)S(1)} all-gather(f32[1,32,16]{1,2,0:T(8,128)S(1)} %get-tuple-element.32), channel_id=1, replica_groups=mesh['groups'=2,'row'=16] {'row'}, dimensions={0}, use_global_device_ids=true | all-gather | bytes 34816 | tf_op jit(solution)/shard_map/all_gather | solution.py:53
  30.6 24.6 %all-reduce = f32[512]{0:T(512)S(1)} all-reduce(f32[512]{0:T(512)S(1)} %convert_dynamic-update-slice_fusion), channel_id=1, replica_groups=mesh['groups'=2,'row'=16] {'row'}, use_global_device_ids=true, to_apply=%add | all-reduce | flops 512 | bytes 4096
  56.2 5.3 %broadcast_multiply_fusion = f32[32,512,128]{2,1,0:T(8,128)S(1)} fusion(f32[32,512,128]{2,1,0:T(8,128)} %param.13, f32[32,512]{1,0:T(8,128)S(1)} %fusion.28), kind=kLoop, calls=%fused_computation.14 | loop fusion | flops 2097152 | bytes 16842752 | tf_op jit(solution)/shard_map/mul | solution.py:61
  61.5 30.1 %fusion.11 = f32[32,256,32,32]{1,3,2,0:T(8,128)} fusion(f32[32,32,128,1]{2,1,0,3:T(8,128)S(1)} %bitcast.100, f32[32,512,128]{2,1,0:T(8,128)S(1)} %broadcast_multiply_fusion), kind=kOutput, calls=%fused_computation.13 | convolution fusion | flops 12884901888 | bytes 38273024 | tf_op jit(solution)/shard_map/rjk,abk->rjab/dot_general | solution.py:67
  91.6 30.2 %fusion.10 = f32[32,256,32,32]{1,3,2,0:T(8,128)} fusion(f32[32,32,128,1]{2,1,0,3:T(8,128)S(1)} %bitcast.101, f32[32,512,128]{2,1,0:T(8,128)S(1)} %broadcast_multiply_fusion), kind=kOutput, calls=%fused_computation.11 | convolution fusion | flops 12884901888 | bytes 38273024 | tf_op jit(solution)/shard_map/rjk,abk->rjab/dot_general | solution.py:67
  123.1 50.2 %fusion.15 = f32[16,256,32]{1,0,2:T(8,128)S(1)} fusion(f32[32,256,32,32]{1,3,2,0:T(8,128)} %fusion.11, f32[32,16,32]{0,2,1:T(8,128)S(1)} %convolution_multiply_fusion), kind=kOutput, calls=%fused_computation.16 | convolution fusion | flops 1610612736 | bytes 34144256 | tf_op jit(solution)/shard_map/rjab,rsa->jsb/dot_general | solution.py:69
  173.3 38.5 %fusion.18 = f32[16,256,32]{1,0,2:T(8,128)S(1)} fusion(f32[32,256,32,32]{1,3,2,0:T(8,128)S(1)} %copy-done.1, f32[32,16,32]{0,2,1:T(8,128)S(1)} %convolution_multiply_fusion), kind=kOutput, calls=%fused_computation.17 | convolution fusion | flops 1610612736 | bytes 34144256 | tf_op jit(solution)/shard_map/rjab,rsa->jsb/dot_general | solution.py:69
  212.7 2.6 collective-permute-done
  217.7 23.9 %collective-permute-done.1 = f32[512,16,32]{0,2,1:T(8,128)} collective-permute-done((f32[512,16,32]{0,2,1:T(8,128)S(1)}, f32[512,16,32]{0,2,1:T(8,128)}, u32[]{:S(2)}, u32[]{:S(2)}) %collective-permute-start.1) | collective-permute-done | bytes 1048608 | tf_op jit(solution)/shard_map/ppermute | solution.py:13
  241.6 1.4 add.28
  243.0 8.5 %collective-permute-start.2 = (f32[512,16,32]{0,2,1:T(8,128)S(1)}, f32[512,16,32]{0,2,1:T(8,128)}, u32[]{:S(2)}, u32[]{:S(2)}) collective-permute-start(f32[512,16,32]{0,2,1:T(8,128)S(1)} %add.28), channel_id=1, source_target_pairs={{0,4},{1,5},{2,6},{3,7},{4,0},{5,1},{6,2},{7,3},{8,12},{9,13},{10,... | collective-permute-start | bytes 3145736 | tf_op jit(solution)/shard_map/ppermute | solution.py:13
  251.6 11.1 %all-gather.3.cloned.1.call-done = f32[512,512]{1,0:T(8,128)} async-done(((f32[32,512]{1,0:T(8,128)}), f32[512,512]{1,0:T(8,128)}) %all-gather.3.cloned.1.call-update) | async-done | bytes 1048592 | tf_op jit(solution)/shard_map/all_gather | solution.py:47
  262.7 2.5 copy.118
  265.2 11.9 %collective-permute-done.2 = f32[512,16,32]{0,2,1:T(8,128)} collective-permute-done((f32[512,16,32]{0,2,1:T(8,128)S(1)}, f32[512,16,32]{0,2,1:T(8,128)}, u32[]{:S(2)}, u32[]{:S(2)}) %collective-permute-start.2) | collective-permute-done | bytes 1048608 | tf_op jit(solution)/shard_map/ppermute | solution.py:13
  277.1 1.4 add.29
  279.3 16.6 %fusion.12 = f32[32,16,32,128]{3,2,0,1:T(8,128)S(1)} fusion(f32[512,16,32,1]{0,2,3,1:T(8,128)} %bitcast.105, f32[32,512,128]{2,1,0:T(8,128)} %copy-done.2), kind=kOutput, calls=%fused_computation.15 | convolution fusion | flops 12884901888 | bytes 17825792 | tf_op jit(solution)/shard_map/rjk,jsc->rsck/dot_general | solution.py:71
  296.0 3.2 copy-done.3
  299.2 10.9 %fusion.25 = f32[32,16,32]{2,1,0:T(8,128)S(1)} fusion(f32[32,16,32,128]{3,2,0,1:T(8,128)S(1)} %fusion.12, f32[32,32,128]{2,1,0:T(8,128)S(1)} %bitcast.102), kind=kOutput, calls=%fused_computation.21 | convolution fusion | flops 805306368 | bytes 8978432 | tf_op jit(solution)/shard_map/rsck,ack->rsa/dot_general | solution.py:73
  310.2 12.7 %fusion.21 = f32[32,32,128]{2,0,1:T(8,128)S(1)} fusion(f32[32,16,32,128]{3,2,0,1:T(8,128)} %copy-done.3, f32[32,16,32]{0,2,1:T(8,128)S(1)} %convolution_multiply_fusion), kind=kOutput, calls=%fused_computation.18 | convolution fusion | flops 805306368 | bytes 8978432 | tf_op jit(solution)/shard_map/rsa,rsck->ack/dot_general | solution.py:72
  330.1 86.8 %all-reduce.5.cloned.1.call-done = f32[1024,128]{1,0:T(8,128)} async-done(((f32[1024,128]{1,0:T(8,128)}), f32[1024,128]{1,0:T(8,128)}) %all-reduce.5.cloned.1.call-update) | async-done | bytes 524304 | tf_op jit(solution)/shard_map/psum | solution.py:92
  416.9 92.3 %all-reduce.7.cloned.1.call-done = (f32[256,32]{0,1:T(8,128)}, f32[256,32]{0,1:T(8,128)}) async-done(((f32[256,32]{0,1:T(8,128)}, f32[256,32]{0,1:T(8,128)}), (f32[256,32]{0,1:T(8,128)}, f32[256,32]{0,1:T(8,128)})) %all-reduce.7.cloned.1.call-update) | async-done | bytes 65552 | tf_op jit(solution)/shard_map/psum | solution.py:92
  509.2 1.4 copy.181
  510.5 1.4 copy.182
  511.9 1.9 copy.183
  (47 shorter events, 17.1 us)
Async XLA Ops:
  7.2 114.6 %copy-start = (f32[16,32,256]{2,1,0:T(8,128)S(1)}, f32[16,32,256]{2,1,0:T(8,128)}, u32[]{:S(2)}) copy-start(f32[16,32,256]{2,1,0:T(8,128)} %param.7) | copy-start | bytes 1572868
  7.2 255.5 %all-gather.3.cloned.1.call-start = ((), (), s32[]{:S(2)}) async-start(), calls=%async_computation | async-start | bytes 1114112 | tf_op jit(solution)/shard_map/all_gather | solution.py:47
  56.2 5.3 %copy-start.4 = (f32[1024,128]{1,0:T(8,128)S(1)}, f32[1024,128]{1,0:T(8,128)}, u32[]{:S(2)}) copy-start(f32[1024,128]{1,0:T(8,128)} %param.12) | copy-start | bytes 1572868
  61.4 30.1 %copy-start.2 = (f32[32,512,128]{2,1,0:T(8,128)}, f32[32,512,128]{2,1,0:T(8,128)S(1)}, u32[]{:S(2)}) copy-start(f32[32,512,128]{2,1,0:T(8,128)S(1)} %broadcast_multiply_fusion) | copy-start | bytes 25165828
  91.6 30.2 %copy-start.5 = (f32[256,32]{0,1:T(8,128)S(1)}, f32[256,32]{0,1:T(8,128)}, u32[]{:S(2)}) copy-start(f32[256,32]{0,1:T(8,128)} %param.10) | copy-start | bytes 98308
  123.1 50.2 %copy-start.1 = (f32[32,256,32,32]{1,3,2,0:T(8,128)S(1)}, f32[32,256,32,32]{1,3,2,0:T(8,128)}, u32[]{:S(2)}) copy-start(f32[32,256,32,32]{1,3,2,0:T(8,128)} %fusion.10) | copy-start | bytes 100663296
  173.3 42.3 %copy-start.6 = (f32[256,32]{0,1:T(8,128)S(1)}, f32[256,32]{0,1:T(8,128)}, u32[]{:S(2)}) copy-start(f32[256,32]{0,1:T(8,128)} %param.11) | copy-start | bytes 98308
  212.6 2.7 collective-permute-start
  215.5 26.1 %collective-permute-start.1 = (f32[512,16,32]{0,2,1:T(8,128)S(1)}, f32[512,16,32]{0,2,1:T(8,128)}, u32[]{:S(2)}, u32[]{:S(2)}) collective-permute-start(f32[512,16,32]{0,2,1:T(8,128)S(1)} %fusion.47), channel_id=1, source_target_pairs={{0,2},{1,3},{2,0},{3,1},{4,6},{5,7},{6,4},{7,5},{8,10},{9,11},{10,... | collective-permute-start | bytes 3145736 | tf_op jit(solution)/shard_map/ppermute | solution.py:13
  217.7 199.2 %all-reduce.5.cloned.1.call-start = ((), (), s32[]{:S(2)}) async-start(), calls=%async_computation.1 | async-start | bytes 1048576 | tf_op jit(solution)/shard_map/psum | solution.py:92
  243.0 34.0 %collective-permute-start.2 = (f32[512,16,32]{0,2,1:T(8,128)S(1)}, f32[512,16,32]{0,2,1:T(8,128)}, u32[]{:S(2)}, u32[]{:S(2)}) collective-permute-start(f32[512,16,32]{0,2,1:T(8,128)S(1)} %add.28), channel_id=1, source_target_pairs={{0,4},{1,5},{2,6},{3,7},{4,0},{5,1},{6,2},{7,3},{8,12},{9,13},{10,... | collective-permute-start | bytes 3145736 | tf_op jit(solution)/shard_map/ppermute | solution.py:13
  278.5 45.6 %collective-permute-start.3 = (f32[512,16,32]{0,2,1:T(8,128)S(1)}, f32[512,16,32]{0,2,1:T(8,128)}, u32[]{:S(2)}, u32[]{:S(2)}) collective-permute-start(f32[512,16,32]{0,2,1:T(8,128)S(1)} %add.29), channel_id=1, source_target_pairs={{0,8},{1,9},{2,10},{3,11},{4,12},{5,13},{6,14},{7,15},{8,0},{9,1},... | collective-permute-start | bytes 3145736 | tf_op jit(solution)/shard_map/ppermute | solution.py:13
  295.9 3.2 copy-start.3
  324.1 185.1 %all-reduce.7.cloned.1.call-start = ((), (), s32[]{:S(2)}) async-start(), calls=%async_computation.2 | async-start | bytes 131072 | tf_op jit(solution)/shard_map/psum | solution.py:92
Sparse Core Ops, SparseCore 0:
  217.8 44.8 all-gather.2
  324.2 92.6 all-reduce.4
  421.0 88.0 all-reduce.6
